TPU v7x, 1024 devices: a whole 4x8x16 slice. The times are simulated.
1024 devices in a mesh: dp: 16 (over z), expert: 64 (over x, y, core).
Axes of the slice: x: 4, y: 8, z: 16, core: 2. Of those that a mesh axis runs over, the one named last changes fastest.
Arguments:
- tokens: bfloat16 [4096, 7168], P('expert', 'dp'), may hold values from -6 to 6
- route_ids: int32 [4096, 8], P('expert'), may hold values from 0 to 255, as said below
- route_weight: bfloat16 [4096, 8], P('expert'), may hold values from 0.099609375 to 1
- out_cot: bfloat16 [4096, 7168], P('expert', 'dp'), may hold values from -6 to 6
- base_codes: bfloat16 [64, 2, 7168, 1024], P('expert', None, 'dp'), may hold values from -4 to 4
- base_scales: float32 [64, 2, 8, 7168], P('expert', None, None, 'dp'), may hold values from 0.004 to 0.03
- adapter_down: bfloat16 [64, 2, 32, 7168], P('expert', None, None, 'dp'), may hold values from -0.25 to 0.25
- adapter_up: bfloat16 [64, 2, 32, 1024], P('expert'), may hold values from -0.29882812 to 0.29882812
- magnitude: float32 [64, 2, 1024], P('expert'), may hold values from 0.5 to 2
- down_codes: bfloat16 [64, 1024, 7168], P('expert', None, 'dp'), may hold values from -4 to 4
- down_scales: float32 [64, 8, 7168], P('expert', None, 'dp'), may hold values from 0.01 to 0.06
Outputs:
- layer_out: bfloat16 [4096, 7168], P('expert', 'dp')
- input_grad: bfloat16 [4096, 7168], P('expert', 'dp')
- grad_adapter_down: float32 [64, 2, 32, 7168], P('expert', None, None, 'dp')
- grad_adapter_up: float32 [64, 2, 32, 1024], P('expert')
- grad_magnitude: float32 [64, 2, 1024], P('expert')
Inputs may be any that keep to these rules, and one draw needn't show every extreme that they name: `route_ids`: each row names 8 different experts. In each aligned block of 64 rows no expert is named by more than 3 rows, and one expert below 64 is named by exactly 3 rows in every block.
All inputs are finite; a program needn't handle non-finite values.
Results may differ from a plain program's by a relative error of at most 0.03.
Values may be sent and summed in bfloat16 or wider, within the bound.
A program may use at most 32 MiB of HBM per device.

v0:
```python
import jax
import jax.numpy as jnp
from jax import lax
from jax.sharding import PartitionSpec as P

FF = 1024
QBLK = 128
FFB = 8
CAP = 3


EPSILON = 1e-06
HIGHEST = lax.Precision.HIGHEST


def finish_forward(pre_act, mag_ratio):
    gate_val = pre_act[:, 0] * mag_ratio[0]
    up_val = pre_act[:, 1] * mag_ratio[1]
    sigmoid_val = jax.nn.sigmoid(gate_val)
    silu_val = gate_val * sigmoid_val
    hidden = (silu_val * up_val).astype(jnp.bfloat16)
    return (hidden, up_val, sigmoid_val, silu_val, gate_val)


def backward_units(unit_grad, up_val, sigmoid_val, silu_val, gate_val):
    gate_grad = unit_grad * up_val * sigmoid_val * (1.0 + gate_val * (1.0 - sigmoid_val))
    up_grad = unit_grad * silu_val
    return jnp.stack([gate_grad, up_grad], axis=1)


def body(
    tokens,
    route_ids,
    route_weight,
    out_cot,
    base_codes,
    base_scales,
    adapter_down,
    adapter_up,
    magnitude,
    down_codes,
    down_scales,
):
    experts = lax.axis_size("expert")
    tok_count = tokens.shape[0]
    local_width = tokens.shape[1]
    slot_total = experts * CAP
    expert_ids = jnp.arange(experts, dtype=jnp.int32)
    matches = route_ids[:, :, None] == expert_ids
    present = jnp.sum(matches.astype(jnp.int32), axis=1)
    weight_of = jnp.sum(
        jnp.where(matches, route_weight.astype(jnp.float32)[:, :, None], 0.0), axis=1
    )
    position = jnp.cumsum(present, axis=0) - present
    slot_ids = jnp.arange(CAP, dtype=jnp.int32)
    choose = (present.T[:, None, :] == 1) & (position.T[:, None, :] == slot_ids[None, :, None])
    select = choose.astype(jnp.bfloat16).reshape(slot_total, tok_count)
    weighted = (
        (choose.astype(jnp.float32) * weight_of.T[:, None, :])
        .astype(jnp.bfloat16)
        .reshape(slot_total, tok_count)
    )
    send_in = jnp.dot(select, tokens, preferred_element_type=jnp.float32).astype(jnp.bfloat16)
    send_cot = jnp.dot(weighted, out_cot, preferred_element_type=jnp.float32).astype(jnp.bfloat16)
    recv_in, recv_cot = (
        lax.all_to_all(
            send_in.reshape(experts, CAP, local_width),
            "expert",
            split_axis=0,
            concat_axis=0,
            tiled=True,
        ),
        lax.all_to_all(
            send_cot.reshape(experts, CAP, local_width),
            "expert",
            split_axis=0,
            concat_axis=0,
            tiled=True,
        ),
    )
    expert_in = recv_in.reshape(slot_total, local_width)
    route_cot = recv_cot.reshape(slot_total, local_width)
    scale_full = jnp.swapaxes(base_scales[0], 1, 2)
    dequant = (
        base_codes[0].astype(jnp.float32).reshape(2, local_width, FFB, QBLK) * scale_full[..., None]
    ).reshape(2, local_width, FF)
    adapted = dequant + jnp.einsum(
        "ird,irf->idf", adapter_down[0], adapter_up[0], preferred_element_type=jnp.float32
    )
    adapted_b = adapted.astype(jnp.bfloat16)
    down_f = adapter_down[0].astype(jnp.float32)
    col_part = jnp.sum(adapted * adapted, axis=1)
    low_part = jnp.einsum(
        "sd,ird->sir", expert_in, adapter_down[0], preferred_element_type=jnp.float32
    )
    proj_part = jnp.einsum("ird,idf->irf", down_f, adapted, precision=HIGHEST)
    col_sq, low_sum, rank_proj = (
        lax.psum(col_part.astype(jnp.bfloat16), "dp").astype(jnp.float32),
        lax.psum(low_part.astype(jnp.bfloat16), "dp").astype(jnp.float32),
        lax.psum(proj_part.astype(jnp.bfloat16), "dp").astype(jnp.float32),
    )
    col_norm = jnp.sqrt(col_sq + EPSILON)
    mag_ratio = magnitude[0] / col_norm
    down_base = (
        (
            down_codes[0].astype(jnp.float32).reshape(FFB, QBLK, local_width)
            * down_scales[0][:, None, :]
        )
        .reshape(FF, local_width)
        .astype(jnp.bfloat16)
    )
    row_block = expert_in
    pre_share = lax.psum_scatter(
        jnp.einsum("sd,idf->sif", row_block, adapted_b, preferred_element_type=jnp.float32).astype(
            jnp.bfloat16
        ),
        "dp",
        scatter_dimension=0,
        tiled=True,
    ).astype(jnp.float32)
    hidden_share, up_val, sigmoid_val, silu_val, gate_val = finish_forward(pre_share, mag_ratio)
    expert_out = jnp.dot(
        lax.all_gather(hidden_share, "dp", axis=0, tiled=True),
        down_base,
        preferred_element_type=jnp.float32,
    ).astype(jnp.bfloat16)
    row_block = route_cot
    unit_share = lax.psum_scatter(
        lax.dot_general(
            row_block, down_base, (((1,), (1,)), ((), ())), preferred_element_type=jnp.float32
        ).astype(jnp.bfloat16),
        "dp",
        scatter_dimension=0,
        tiled=True,
    ).astype(jnp.float32)
    pre_grad = backward_units(unit_share, up_val, sigmoid_val, silu_val, gate_val)
    mag_grad = lax.psum(jnp.sum(pre_grad * pre_share, axis=0) / col_norm, "dp")
    scaled = lax.all_gather(
        (pre_grad * mag_ratio[None]).astype(jnp.bfloat16), "dp", axis=0, tiled=True
    )
    shrink = magnitude[0] * mag_grad / (col_norm * col_norm)
    slot_grad = jnp.einsum(
        "sif,idf->sd", scaled, adapted_b, preferred_element_type=jnp.float32
    ).astype(jnp.bfloat16)
    rank_back = jnp.einsum(
        "sif,irf->sir", scaled, adapter_up[0], preferred_element_type=jnp.float32
    ).astype(jnp.bfloat16)
    grad_down = jnp.einsum("sir,sd->ird", rank_back, expert_in, preferred_element_type=jnp.float32)
    grad_down = grad_down - jnp.einsum(
        "irf,idf->ird",
        adapter_up[0].astype(jnp.float32) * shrink[:, None, :],
        adapted,
        precision=HIGHEST,
    )
    grad_up = jnp.einsum(
        "sir,sif->irf", low_sum.astype(jnp.bfloat16), scaled, preferred_element_type=jnp.float32
    )
    grad_up = grad_up - rank_proj * shrink[:, None, :]
    out_back, grad_back = (
        lax.all_to_all(
            expert_out.reshape(experts, CAP, local_width),
            "expert",
            split_axis=0,
            concat_axis=0,
            tiled=True,
        ),
        lax.all_to_all(
            slot_grad.reshape(experts, CAP, local_width),
            "expert",
            split_axis=0,
            concat_axis=0,
            tiled=True,
        ),
    )
    layer_out = lax.dot_general(
        weighted,
        out_back.reshape(slot_total, local_width),
        (((0,), (0,)), ((), ())),
        preferred_element_type=jnp.float32,
    ).astype(jnp.bfloat16)
    input_grad = lax.dot_general(
        select,
        grad_back.reshape(slot_total, local_width),
        (((0,), (0,)), ((), ())),
        preferred_element_type=jnp.float32,
    ).astype(jnp.bfloat16)
    return (layer_out, input_grad, grad_down[None], grad_up[None], mag_grad[None])


def solution(mesh):
    in_specs = (
        P("expert", "dp"),
        P("expert", None),
        P("expert", None),
        P("expert", "dp"),
        P("expert", None, "dp", None),
        P("expert", None, None, "dp"),
        P("expert", None, None, "dp"),
        P("expert", None, None, None),
        P("expert", None, None),
        P("expert", None, "dp"),
        P("expert", None, "dp"),
    )
    out_specs = (
        P("expert", "dp"),
        P("expert", "dp"),
        P("expert", None, None, "dp"),
        P("expert", None, None, None),
        P("expert", None, None),
    )
    return jax.shard_map(body, mesh=mesh, in_specs=in_specs, out_specs=out_specs, check_vma=False)
```

profile of v0, /device:TPU:1, one launch (start us, length us, event | category | flops | bytes accessed | tf_op | source)
XLA Modules:
  0.0 367.3 jit_solution(13448577609847538905)
XLA Ops:
  11.1 18.3 %all-to-all-start = ((bf16[64,3,448]{2,1,0:T(4,128)(2,1)}), bf16[64,3,448]{2,1,0:T(4,128)(2,1)S(1)}, u32[]{:S(2)}, u32[]{:S(2)}) async-start(bf16[64,3,448]{2,1,0:T(4,128)(2,1)} %reshape.79), calls=%async_computation | async-start | bytes 524288 | tf_op jit(solution)/shard_map/all_to_all | solution.py:66
  33.4 2.4 mul.122
  35.8 4.8 %mul.123 = f32[2,448,1024]{2,1,0:T(8,128)} reshape(f32[2,448,8,128]{3,2,1,0:T(8,128)} %mul.122) | data formatting | bytes 7340032 | tf_op jit(solution)/shard_map/mul | solution.py:85
  42.1 4.7 %multiply_reduce_fusion = (bf16[2,1024]{1,0:T(2,128)(2,1)S(1)}, f32[2,448,1024]{2,1,0:T(8,128)}) fusion(bf16[1,2,32,1024]{3,2,1,0:T(8,128)(2,1)S(1)} %copy-done.3, bf16[1,2,32,448]{3,2,1,0:T(8,128)(2,1)S(1)} %copy-done, f32[2,448,1024]{2,1,0:T(8,128)} %mul.123, bf16[1,2,448,1024]{3,2,1,0:T(8,128)(2,1)S(1)} %copy-done.2), kind=kOutput, calls=%fused_computation.2 | convolution fusion | flops 63305728 | bytes 9367552 | tf_op jit(solution)/shard_map/ird,irf->idf/dot_general | solution.py:87
  50.5 4.1 %fusion.8 = bf16[2,32,1024]{2,1,0:T(8,128)(2,1)} fusion(f32[2,448,1024]{2,1,0:T(8,128)} %get-tuple-element.21, bf16[1,2,32,448]{3,2,1,0:T(8,128)(2,1)S(1)} %copy-done), kind=kOutput, calls=%fused_computation.23 | convolution fusion | flops 352387072 | bytes 3858432 | tf_op jit(solution)/shard_map/ird,idf->irf/dot_general | solution.py:96
  54.6 10.4 %all-to-all-start.2 = ((bf16[64,3,448]{2,1,0:T(4,128)(2,1)}), bf16[64,3,448]{2,1,0:T(4,128)(2,1)S(1)}, u32[]{:S(2)}, u32[]{:S(2)}) async-start(bf16[64,3,448]{2,1,0:T(4,128)(2,1)} %reshape.82), calls=%async_computation.2 | async-start | bytes 524288 | tf_op jit(solution)/shard_map/all_to_all | solution.py:73
  65.3 2.7 convolution_convert_fusion
  68.0 1.7 copy.75
  69.7 7.4 %all-to-all-done.2 = bf16[64,3,448]{2,1,0:T(4,128)(2,1)S(1)} async-done(((bf16[64,3,448]{2,1,0:T(4,128)(2,1)}), bf16[64,3,448]{2,1,0:T(4,128)(2,1)S(1)}, u32[]{:S(2)}, u32[]{:S(2)}) %all-to-all-start.2) | async-done | bytes 172064 | tf_op jit(solution)/shard_map/all_to_all | solution.py:73
  77.6 33.6 %fusion = bf16[16,1024]{1,0:T(8,128)(2,1)S(1)} fusion(bf16[192,1024]{1,0:T(8,128)(2,1)S(1)} %convolution_convert_fusion.1), kind=kCustom, calls=%all-reduce-scatter | all-reduce-scatter fusion | flops 262145 | bytes 430080
  111.2 2.5 collective-permute-start
  113.7 2.0 collective-permute-start.1
  115.7 3.2 collective-permute-start.2
  118.9 5.2 %collective-permute-start.3 = (bf16[12,1024]{1,0:T(8,128)(2,1)S(1)}, bf16[12,1024]{1,0:T(8,128)(2,1)S(1)}, u32[]{:S(2)}, u32[]{:S(2)}) collective-permute-start(bf16[12,1024]{1,0:T(8,128)(2,1)S(1)} %slice.20), channel_id=1, source_target_pairs={{0,256},{64,320},{128,384},{192,448},{256,512},{320,576},{384,640}... | collective-permute-start | bytes 73736
  124.3 42.9 %all-reduce.3 = (bf16[2,1024]{1,0:T(2,128)(2,1)S(1)}, bf16[192,2,32]{0,2,1:T(8,128)(2,1)}) all-reduce(bf16[2,1024]{1,0:T(2,128)(2,1)S(1)} %get-tuple-element.20, bf16[192,2,32]{0,2,1:T(8,128)(2,1)S(1)} %convolution_convert_fusion.6), channel_id=1, replica_groups=mesh['dp'=16,'expert'=64] {'dp'}, use_global_device_ids=true, to_apply=%region_5.6 | all-reduce | flops 14336 | bytes 57344 | tf_op jit(solution)/shard_map/psum | solution.py:98
  167.9 43.5 %all-reduce.7.cloned.1.call-done = (bf16[192,2,1024]{2,1,0:T(2,128)(2,1)}, bf16[2,32,1024]{2,1,0:T(8,128)(2,1)}) async-done(((bf16[192,2,1024]{2,1,0:T(2,128)(2,1)}, bf16[2,32,1024]{2,1,0:T(8,128)(2,1)}), (bf16[192,2,1024]{2,1,0:T(2,128)(2,1)}, bf16[2,32,1024]{2,1,0:T(8,128)(2,1)})) %all-reduce.7.cloned.1.call-update) | async-done | bytes 917520
  213.5 22.3 %psum.29 = f32[2,1024]{1,0:T(2,128)S(1)} all-reduce(f32[2,1024]{1,0:T(2,128)S(1)} %fusion.59), channel_id=1, replica_groups=mesh['dp'=16,'expert'=64] {'dp'}, use_global_device_ids=true, to_apply=%region_8.9 | all-reduce | flops 2048 | bytes 16384 | tf_op jit(solution)/shard_map/psum | solution.py:137
  236.4 24.5 %all_gather.7 = bf16[192,2,1024]{2,1,0:T(2,128)(2,1)S(1)} all-gather(bf16[12,2,1024]{2,1,0:T(2,128)(2,1)S(1)} %get-tuple-element.13), channel_id=1, replica_groups=mesh['dp'=16,'expert'=64] {'dp'}, dimensions={0}, use_global_device_ids=true | all-gather | bytes 835584 | tf_op jit(solution)/shard_map/all_gather | solution.py:138
  260.9 2.8 fusion.5
  264.5 33.5 %all-to-all-start.3 = ((bf16[64,3,448]{2,1,0:T(4,128)(2,1)}), bf16[64,3,448]{2,1,0:T(4,128)(2,1)S(1)}, u32[]{:S(2)}, u32[]{:S(2)}) async-start(bf16[64,3,448]{2,1,0:T(4,128)(2,1)} %reshape.84), calls=%async_computation.3 | async-start | bytes 524288 | tf_op jit(solution)/shard_map/all_to_all | solution.py:167
  298.1 24.3 %all-gather = bf16[16,12,1024]{2,1,0:T(8,128)(2,1)S(1)} all-gather(bf16[1,12,1024]{2,1,0:T(8,128)(2,1)S(1)} %get-tuple-element.11), channel_id=1, replica_groups=mesh['dp'=16,'expert'=64] {'dp'}, dimensions={0}, use_global_device_ids=true | all-gather | bytes 417792 | tf_op jit(solution)/shard_map/all_gather | solution.py:123
  324.5 5.3 %fusion.21 = f32[2,32,448]{2,1,0:T(8,128)S(1)} fusion(f32[2,448,1024]{2,1,0:T(8,128)} %get-tuple-element.21, bf16[1,2,32,1024]{3,2,1,0:T(8,128)(2,1)S(1)} %copy-done.3, f32[2,1024]{1,0:T(2,128)S(1)} %copy-done.8), kind=kOutput, calls=%fused_computation.36 | convolution fusion | flops 352452608 | bytes 3923968 | tf_op jit(solution)/shard_map/irf,idf->ird/dot_general | solution.py:149
  330.9 16.7 %all-to-all-start.1 = ((bf16[64,3,448]{2,1,0:T(4,128)(2,1)}), bf16[64,3,448]{2,1,0:T(4,128)(2,1)S(1)}, u32[]{:S(2)}, u32[]{:S(2)}) async-start(bf16[64,3,448]{2,1,0:T(4,128)(2,1)} %reshape.81), calls=%async_computation.1 | async-start | bytes 524288 | tf_op jit(solution)/shard_map/all_to_all | solution.py:160
  349.6 10.1 %all-to-all-done.1 = bf16[64,3,448]{2,1,0:T(4,128)(2,1)S(1)} async-done(((bf16[64,3,448]{2,1,0:T(4,128)(2,1)}), bf16[64,3,448]{2,1,0:T(4,128)(2,1)S(1)}, u32[]{:S(2)}, u32[]{:S(2)}) %all-to-all-start.1) | async-done | bytes 172064 | tf_op jit(solution)/shard_map/all_to_all | solution.py:160
  (90 shorter events, 22.7 us)
Async XLA Ops:
  7.2 34.9 %copy-start = (bf16[1,2,32,448]{3,2,1,0:T(8,128)(2,1)S(1)}, bf16[1,2,32,448]{3,2,1,0:T(8,128)(2,1)}, u32[]{:S(2)}) copy-start(bf16[1,2,32,448]{3,2,1,0:T(8,128)(2,1)} %param.17) | copy-start | bytes 172036
  8.5 0.6 copy-start.6
  11.1 22.1 %copy-start.13 = (f32[1,2,8,448]{3,2,1,0:T(8,128)S(1)}, f32[1,2,8,448]{3,2,1,0:T(8,128)}, u32[]{:S(2)}) copy-start(f32[1,2,8,448]{3,2,1,0:T(8,128)} %param.16) | copy-start | bytes 86020
  11.1 43.5 %all-to-all-start = ((bf16[64,3,448]{2,1,0:T(4,128)(2,1)}), bf16[64,3,448]{2,1,0:T(4,128)(2,1)S(1)}, u32[]{:S(2)}, u32[]{:S(2)}) async-start(bf16[64,3,448]{2,1,0:T(4,128)(2,1)} %reshape.79), calls=%async_computation | async-start | bytes 524288 | tf_op jit(solution)/shard_map/all_to_all | solution.py:66
  35.8 6.3 %copy-start.3 = (bf16[1,2,32,1024]{3,2,1,0:T(8,128)(2,1)S(1)}, bf16[1,2,32,1024]{3,2,1,0:T(8,128)(2,1)}, u32[]{:S(2)}) copy-start(bf16[1,2,32,1024]{3,2,1,0:T(8,128)(2,1)} %param.18) | copy-start | bytes 393220
  40.6 1.5 copy-start.2
  42.1 4.7 %copy-start.9 = (bf16[64,448]{1,0:T(8,128)(2,1)S(1)}, bf16[64,448]{1,0:T(8,128)(2,1)}, u32[]{:S(2)}) copy-start(bf16[64,448]{1,0:T(8,128)(2,1)} %param.14) | copy-start | bytes 172036
  54.6 22.4 %all-to-all-start.2 = ((bf16[64,3,448]{2,1,0:T(4,128)(2,1)}), bf16[64,3,448]{2,1,0:T(4,128)(2,1)S(1)}, u32[]{:S(2)}, u32[]{:S(2)}) async-start(bf16[64,3,448]{2,1,0:T(4,128)(2,1)} %reshape.82), calls=%async_computation.2 | async-start | bytes 524288 | tf_op jit(solution)/shard_map/all_to_all | solution.py:73
  65.1 12.1 %copy-start.4 = (bf16[8,128,448]{1,0,2:T(8,128)(2,1)S(1)}, bf16[8,128,448]{1,0,2:T(8,128)(2,1)}, u32[]{:S(2)}) copy-start(bf16[8,128,448]{1,0,2:T(8,128)(2,1)} %fusion.4) | copy-start | bytes 2752516
  65.1 146.3 %all-reduce.7.cloned.1.call-start = ((), (), s32[]{:S(2)}) async-start(), calls=%async_computation.4 | async-start | bytes 1835008
  67.9 99.3 %copy-start.11 = (f32[1,2,1024]{2,1,0:T(2,128)S(1)}, f32[1,2,1024]{2,1,0:T(2,128)}, u32[]{:S(2)}) copy-start(f32[1,2,1024]{2,1,0:T(2,128)} %param.19) | copy-start | bytes 24580
  111.2 56.1 %collective-permute-start = (bf16[16,1024]{1,0:T(8,128)(2,1)S(1)}, bf16[16,1024]{1,0:T(8,128)(2,1)S(1)}, u32[]{:S(2)}, u32[]{:S(2)}) collective-permute-start(bf16[16,1024]{1,0:T(8,128)(2,1)S(1)} %fusion), channel_id=1, source_target_pairs={{0,64},{64,128},{128,192},{192,256},{256,320},{320,384},{384,448},... | collective-permute-start | bytes 98312
  113.7 53.6 %collective-permute-start.1 = (bf16[16,1024]{1,0:T(8,128)(2,1)S(1)}, bf16[16,1024]{1,0:T(8,128)(2,1)S(1)}, u32[]{:S(2)}, u32[]{:S(2)}) collective-permute-start(bf16[16,1024]{1,0:T(8,128)(2,1)S(1)} %fusion), channel_id=1, source_target_pairs={{0,128},{64,192},{128,256},{192,320},{256,384},{320,448},{384,512}... | collective-permute-start | bytes 98312
  115.7 51.6 %collective-permute-start.2 = (bf16[16,1024]{1,0:T(8,128)(2,1)S(1)}, bf16[16,1024]{1,0:T(8,128)(2,1)S(1)}, u32[]{:S(2)}, u32[]{:S(2)}) collective-permute-start(bf16[16,1024]{1,0:T(8,128)(2,1)S(1)} %fusion), channel_id=1, source_target_pairs={{0,192},{64,256},{128,320},{192,384},{256,448},{320,512},{384,576}... | collective-permute-start | bytes 98312
  118.9 48.3 %collective-permute-start.3 = (bf16[12,1024]{1,0:T(8,128)(2,1)S(1)}, bf16[12,1024]{1,0:T(8,128)(2,1)S(1)}, u32[]{:S(2)}, u32[]{:S(2)}) collective-permute-start(bf16[12,1024]{1,0:T(8,128)(2,1)S(1)} %slice.20), channel_id=1, source_target_pairs={{0,256},{64,320},{128,384},{192,448},{256,512},{320,576},{384,640}... | collective-permute-start | bytes 73736
  235.8 0.6 copy-start.12
  260.9 62.1 %copy-start.1 = (bf16[1,1024,448]{1,2,0:T(8,128)(2,1)S(1)}, bf16[1,1024,448]{1,2,0:T(8,128)(2,1)}, u32[]{:S(2)}) copy-start(bf16[1,1024,448]{1,2,0:T(8,128)(2,1)} %param.20) | copy-start | bytes 2752516
  264.5 66.4 %all-to-all-start.3 = ((bf16[64,3,448]{2,1,0:T(4,128)(2,1)}), bf16[64,3,448]{2,1,0:T(4,128)(2,1)S(1)}, u32[]{:S(2)}, u32[]{:S(2)}) async-start(bf16[64,3,448]{2,1,0:T(4,128)(2,1)} %reshape.84), calls=%async_computation.3 | async-start | bytes 524288 | tf_op jit(solution)/shard_map/all_to_all | solution.py:167
  322.5 2.0 copy-start.8
  323.6 24.0 %copy-start.5 = (bf16[2,32,1024]{2,1,0:T(8,128)(2,1)S(1)}, bf16[2,32,1024]{2,1,0:T(8,128)(2,1)}, u32[]{:S(2)}) copy-start(bf16[2,32,1024]{2,1,0:T(8,128)(2,1)} %get-tuple-element.8) | copy-start | bytes 393220
  323.6 24.0 %copy-start.10 = (bf16[192,2,32]{0,2,1:T(8,128)(2,1)S(1)}, bf16[192,2,32]{0,2,1:T(8,128)(2,1)}, u32[]{:S(2)}) copy-start(bf16[192,2,32]{0,2,1:T(8,128)(2,1)} %get-tuple-element.6) | copy-start | bytes 73732
  323.7 25.1 %copy-start.7 = (pred[64,64]{1,0:T(8,128)(4,1)S(1)}, pred[64,64]{1,0:T(8,128)(4,1)}, u32[]{:S(2)}) copy-start(pred[64,64]{1,0:T(8,128)(4,1)} %copy-done.6) | copy-start | bytes 12292
  330.9 28.7 %all-to-all-start.1 = ((bf16[64,3,448]{2,1,0:T(4,128)(2,1)}), bf16[64,3,448]{2,1,0:T(4,128)(2,1)S(1)}, u32[]{:S(2)}, u32[]{:S(2)}) async-start(bf16[64,3,448]{2,1,0:T(4,128)(2,1)} %reshape.81), calls=%async_computation.1 | async-start | bytes 524288 | tf_op jit(solution)/shard_map/all_to_all | solution.py:160
Sparse Core Ops, SparseCore 0:
  77.7 133.6 all-reduce.6
where the time goes:
time: 368 us; the launch traced here: 367 us
  blocking collectives  148 us (40%)
  starting transfers between devices  92 us (25%)
  waiting for transfers between devices  60.9 us (17%)
  matrix products  25.7 us (7%)
  local copies, waits for them, and re-layouts  19.3 us (5%)
  between operations  15.8 us (4%)
  other arithmetic  5.97 us (2%)
    unnamed x6, waiting for transfers between devices  43.5 us
    psum x1, blocking collectives, body(): lax.psum(col_part.astype(jnp.bfloat16), 'dp').astype(jnp.float32)  42.9 us
    unnamed x1, blocking collectives  33.6 us
    all_to_all x1, starting transfers between devices, body(): lax.all_to_all(slot_grad.reshape(experts, CAP, local_width), 'expert', sp...  33.5 us
    all_gather x1, blocking collectives, body(): lax.all_gather((pre_grad * mag_ratio[None]).astype(jnp.bfloat16), 'dp', a...  24.5 us
    all_gather x1, blocking collectives, body(): lax.all_gather(hidden_share, 'dp', axis=0, tiled=True)  24.3 us
    psum x1, blocking collectives, body(): mag_grad = lax.psum(jnp.sum(pre_grad * pre_share, axis=0) / col_norm, 'dp')  22.3 us
    all_to_all x1, starting transfers between devices, body(): lax.all_to_all(send_in.reshape(experts, CAP, local_width), 'expert', spli...  18.3 us
  transfers between devices with their start and end apart: 9, of which 3 were waited for; matrix products, arithmetic and copies ran while one was open for 20% of the time, Pallas kernels for 0%

commit v1 on v0

v1 whole, which is shorter than its diff:
```python
import jax
import jax.numpy as jnp
from jax import lax
from jax.experimental import pallas as pl
from jax.experimental.pallas import tpu as pltpu
from jax.sharding import PartitionSpec as P

EPSILON = 1e-06
MESH = pl.DeviceIdType.MESH
F32 = jnp.float32
BF16 = jnp.bfloat16
NZ = 16
NE = 64
RS_ROWS = 304
AG_ROWS = 352
RS_SUBS = ((0, 96), (96, 96), (192, 112))
AG_SUBS = ((0, 112), (112, 112), (224, 128))
NSUB = 3


def nn(a, b):
    return jnp.dot(a, b, preferred_element_type=F32)


def nt(a, b):
    return lax.dot_general(a, b, (((1,), (1,)), ((), ())), preferred_element_type=F32)


def iota(shape, dim):
    return lax.broadcasted_iota(jnp.int32, shape, dim)


def split(v):
    hi = v.astype(BF16)
    return hi, (v - hi.astype(F32)).astype(BF16)


def kernel(
    tok_ref,
    ids_ref,
    w_ref,
    cot_ref,
    codes_hbm,
    scales_ref,
    down_ref,
    up_ref,
    mag_ref,
    dcodes_hbm,
    dscales_ref,
    layer_ref,
    igrad_ref,
    gdown_ref,
    gup_ref,
    gmag_ref,
    codes,
    dcodes,
    hi,
    lo,
    dbase,
    xin,
    tpose,
    upad,
    perm,
    gt_ref,
    colsq,
    dpad,
    send1,
    recv1,
    send2,
    recv2,
    xs,
    cs,
    yback,
    eown,
    erecv,
    own,
    rbuf,
    lbuf,
    ag,
    hid,
    sgu,
    lowt,
    rank,
    wsem,
    s1s,
    s1r,
    s2s,
    s2r,
    es,
    er,
    rrs,
    rrr,
    rls,
    rlr,
    ars,
    arr,
    als,
    alr,
):
    me = lax.axis_index("expert")
    z = lax.axis_index("dp")
    mx = lax.div(me, 16)
    my = lax.rem(lax.div(me, 2), 8)
    mc = lax.rem(me, 2)
    right = lax.rem(z + 1, NZ)
    left = lax.rem(z + NZ - 1, NZ)

    def peer_of(k):
        px = lax.rem(mx + lax.div(k, 16), 4)
        py = lax.rem(my + lax.rem(lax.div(k, 2), 8), 8)
        pc = lax.rem(mc + lax.rem(k, 2), 2)
        return (px * 8 + py) * 2 + pc

    wcopy = pltpu.make_async_copy(codes_hbm, codes, wsem.at[0])
    dcopy = pltpu.make_async_copy(dcodes_hbm, dcodes, wsem.at[1])
    wcopy.start()
    dcopy.start()

    barrier = pltpu.get_barrier_semaphore()

    @pl.loop(1, NE)
    def _(k):
        pl.semaphore_signal(
            barrier, inc=1, device_id={"expert": peer_of(k)}, device_id_type=MESH
        )

    @pl.loop(1, NZ)
    def _(k):
        pl.semaphore_signal(
            barrier, inc=1, device_id={"dp": lax.rem(z + k, NZ)}, device_id_type=MESH
        )

    ids2 = jnp.concatenate([ids_ref[...], ids_ref[...]], axis=0)
    w2 = jnp.concatenate([w_ref[...], w_ref[...]], axis=0).astype(F32)
    shape = (128, 512)
    col = iota(shape, 1)
    exp_of = lax.shift_right_logical(col, 3)
    present = jnp.zeros(shape, F32)
    wt = jnp.zeros(shape, F32)
    for k in range(8):
        match = ids2[:, k : k + 1] == exp_of
        present = present + jnp.where(match, 1.0, 0.0)
        wt = wt + jnp.where(match, w2[:, k : k + 1], 0.0)
    ti = iota((128, 128), 0)
    tj = iota((128, 128), 1)
    tri = jnp.where((tj < ti) & ((tj >= 64) == (ti >= 64)), 1.0, 0.0).astype(BF16)
    position = nn(tri, present.astype(BF16))
    lane_c = (col & 3).astype(F32)
    choose = jnp.where((present > 0.5) & (position == lane_c), 1.0, 0.0)
    chosen_w = choose * wt
    row_low = iota(shape, 0) < 64
    j_low = (col & 7) < 4
    dt = jnp.where(row_low, jnp.where(j_low, choose, 0.0), jnp.where(j_low, 0.0, chosen_w))
    gt = jnp.where(row_low, jnp.where(j_low, chosen_w, 0.0), jnp.where(j_low, 0.0, choose))
    gt_ref[...] = gt.astype(BF16)

    xin[:, 384:512] = jnp.zeros((128, 128), BF16)
    xin[0:64, 0:448] = tok_ref[...]
    xin[64:128, 0:448] = cot_ref[...]
    disp = nn(dt.T.astype(BF16), xin[...])
    s0 = disp[:, 0:256].reshape(NE, 8, 256)
    s1 = disp[:, 256:512].reshape(NE, 8, 256)
    send1[...] = jnp.concatenate([s0, s1], axis=1).reshape(NE * 16, 256).astype(BF16).reshape(NE, 16, 256)

    pl.semaphore_wait(barrier, NE - 1 + NZ - 1)

    def exchange(src, dst, ssem, rsem):
        def copy(k, slot, peer):
            return pltpu.make_async_remote_copy(
                src_ref=src.at[peer],
                dst_ref=dst.at[slot],
                send_sem=ssem.at[k],
                recv_sem=rsem.at[slot],
                device_id={"expert": peer},
                device_id_type=MESH,
            )

        @pl.loop(1, NE)
        def _(k):
            copy(k, me, peer_of(k)).start()

        dst[me] = src[me]

        def wait():
            @pl.loop(1, NE)
            def _(k):
                peer = peer_of(k)
                copy(k, peer, peer).wait_recv()

        def drain():
            @pl.loop(1, NE)
            def _(k):
                copy(k, me, peer_of(k)).wait_send()

        return wait, drain

    wait1, drain1 = exchange(send1, recv1, s1s, s1r)

    tpose[80:128, :] = jnp.zeros((48, 512), F32)
    tpose[0:80, 384:512] = jnp.zeros((80, 128), F32)
    tpose[0:16, 0:448] = scales_ref[...]
    tpose[16:80, 0:448] = down_ref[...].astype(F32)
    dpad[:, 384:512] = jnp.zeros((64, 128), BF16)
    dpad[:, 0:448] = down_ref[...]
    turned = tpose[...].T
    for i in range(4):
        tpose[:, i * 128 : (i + 1) * 128] = turned[i * 128 : (i + 1) * 128, :]
    upad[...] = jnp.zeros((2, 128, 1024), BF16)
    upad[0, 16:48, :] = up_ref[0]
    upad[1, 48:80, :] = up_ref[1]
    hi[:, 448:512, :] = jnp.zeros((2, 64, 1024), BF16)
    lo[:, 448:512, :] = jnp.zeros((2, 64, 1024), BF16)
    colsq[...] = jnp.zeros((16, 1024), F32)
    wcopy.wait()

    for blk in range(7):
        d0 = blk * 64
        lane0 = (d0 // 128) * 128
        row0 = d0 % 128
        turn = tpose[row0 : row0 + 64, lane0 : lane0 + 128]
        turn_b = turn.astype(BF16)
        for i in range(2):
            for fb in range(8):
                f0 = fb * 128
                scale = turn[:, i * 8 + fb : i * 8 + fb + 1]
                val = codes[i, d0 : d0 + 64, f0 : f0 + 128].astype(F32) * scale
                val = val + nn(turn_b, upad[i, :, f0 : f0 + 128])
                top, bottom = split(val)
                hi[i, d0 : d0 + 64, f0 : f0 + 128] = top
                lo[i, d0 : d0 + 64, f0 : f0 + 128] = bottom
                sq = (val * val).reshape(8, 8, 128).sum(axis=0)
                colsq[i * 8 : i * 8 + 8, f0 : f0 + 128] = colsq[i * 8 : i * 8 + 8, f0 : f0 + 128] + sq

    for q in range(8):
        f0 = q * 128
        c0 = jnp.sum(colsq[0:8, f0 : f0 + 128], axis=0, keepdims=True)
        c1 = jnp.sum(colsq[8:16, f0 : f0 + 128], axis=0, keepdims=True)
        rows = iota((16, 128), 0)
        cblock = jnp.where(rows == 0, c0, jnp.where(rows == 1, c1, 0.0)).astype(BF16)
        for h in range(2):
            dn = dpad[h * 32 : (h + 1) * 32, :]
            proj = nn(dn, hi[h, :, f0 : f0 + 128]) + nn(dn, lo[h, :, f0 : f0 + 128])
            eown[2 * q + h, 0:32, :] = proj.astype(BF16)
            eown[2 * q + h, 32:48, :] = cblock

    def early(k, slot, peer):
        return pltpu.make_async_remote_copy(
            src_ref=eown.at[peer],
            dst_ref=erecv.at[slot],
            send_sem=es.at[k],
            recv_sem=er.at[slot],
            device_id={"dp": peer},
            device_id_type=MESH,
        )

    @pl.loop(1, NZ)
    def _(k):
        early(k, z, lax.rem(z + k, NZ)).start()

    dcopy.wait()
    dbase[:, 384:512] = jnp.zeros((1024, 128), BF16)
    for fb in range(8):
        f0 = fb * 128
        dbase[f0 : f0 + 128, 0:448] = (
            dcodes[f0 : f0 + 128, :].astype(F32) * dscales_ref[fb : fb + 1, :]
        ).astype(BF16)

    pr = iota((512, 512), 0)
    pc = iota((512, 512), 1)

    def target(v):
        return (
            16 * (v & 31)
            + (lax.shift_right_logical(v, 5) & 3)
            + 8 * (lax.shift_right_logical(v, 7) & 1)
            + 4 * lax.shift_right_logical(v, 8)
        )

    perm[0] = jnp.where(pc == target(pr), 1.0, 0.0).astype(BF16)
    perm[1] = jnp.where(pr == target(pc), 1.0, 0.0).astype(BF16)
    for p in range(8, NZ):
        own[p, 288:304, :] = jnp.zeros((16, 128), BF16)

    wait1()
    for h in range(2):
        block = recv1[h * 32 : (h + 1) * 32].reshape(512, 256)
        got = nn(perm[0], block).astype(BF16)
        xs[h, :, 0:256] = got[0:128]
        xs[h, :, 256:512] = got[128:256]
        cs[h, :, 0:256] = got[256:384]
        cs[h, :, 256:512] = got[384:512]

    low = nt(dpad[...], xs[...].reshape(256, 512)).astype(BF16)
    for p in range(8):
        own[p, 288:304, :] = low[(p // 2) * 16 : (p // 2) * 16 + 16, (p % 2) * 128 : (p % 2) * 128 + 128]
    for q in range(8):
        f0 = q * 128
        for h in range(2):
            p = 2 * q + h
            own[p, 0:96, :] = nn(xs[h, 0:96, :], hi[0, :, f0 : f0 + 128]).astype(BF16)
            own[p, 96:192, :] = nn(xs[h, 0:96, :], hi[1, :, f0 : f0 + 128]).astype(BF16)
            own[p, 192:288, :] = nt(cs[h, 0:96, :], dbase[f0 : f0 + 128, :]).astype(BF16)

    def hop(src, dst, ssem, rsem, to):
        return pltpu.make_async_remote_copy(
            src_ref=src,
            dst_ref=dst,
            send_sem=ssem,
            recv_sem=rsem,
            device_id={"dp": to},
            device_id_type=MESH,
        )

    def rs_copy(t, sub, rightward, first):
        r0, n = RS_SUBS[sub]
        buf, ssem, rsem, to = (rbuf, rrs, rrr, right) if rightward else (lbuf, rls, rlr, left)
        chunk = lax.rem(z + 7 - t, NZ) if rightward else lax.rem(z + 8 + t, NZ)
        src = own.at[chunk, pl.ds(r0, n), :] if first else buf.at[t - 1, pl.ds(r0, n), :]
        return chunk, hop(
            src, buf.at[t, pl.ds(r0, n), :], ssem.at[t * NSUB + sub], rsem.at[t * NSUB + sub], to
        )

    for sub in range(NSUB):
        for rightward in (True, False):
            rs_copy(0, sub, rightward, True)[1].start()

    def rs_step(t, rightward, sub):
        r0, n = RS_SUBS[sub]
        buf = rbuf if rightward else lbuf
        rs_copy(t - 1, sub, rightward, True)[1].wait_recv()
        chunk, copy = rs_copy(t, sub, rightward, False)
        buf[t - 1, pl.ds(r0, n), :] = (
            buf[t - 1, pl.ds(r0, n), :].astype(F32) + own[chunk, pl.ds(r0, n), :].astype(F32)
        ).astype(BF16)
        copy.start()

    @pl.loop(1, 7)
    def _(t):
        for sub in range(NSUB):
            for rightward in (True, False):
                rs_step(t, rightward, sub)

    for sub in range(NSUB):
        rs_step(7, False, sub)

    @pl.loop(1, NZ)
    def _(k):
        peer = lax.rem(z + k, NZ)
        early(k, peer, peer).wait_recv()

    erecv[z] = eown[z]
    esum = erecv[0].astype(F32)
    for p in range(1, NZ):
        esum = esum + erecv[p].astype(F32)
    q_lane = pl.multiple_of(lax.div(z, 2) * 128, 128)
    mag = mag_ref[:, pl.ds(q_lane, 128)]
    norm = jnp.sqrt(esum[32:34, :] + EPSILON)
    ratio = mag / norm

    for sub in range(NSUB):
        rs_copy(6, sub, True, True)[1].wait_recv()
        rs_copy(7, sub, False, True)[1].wait_recv()
    total = own[z].astype(F32) + rbuf[6].astype(F32) + lbuf[7].astype(F32)
    gate_pre, up_pre, unit = total[0:96], total[96:192], total[192:288]
    gate_val = gate_pre * ratio[0:1]
    up_val = up_pre * ratio[1:2]
    sig = jax.nn.sigmoid(gate_val)
    silu = gate_val * sig
    gate_grad = unit * up_val * sig * (1.0 + gate_val * (1.0 - sig))
    up_grad = unit * silu
    gm0 = jnp.sum(gate_grad * gate_pre, axis=0, keepdims=True) / norm[0:1]
    gm1 = jnp.sum(up_grad * up_pre, axis=0, keepdims=True) / norm[1:2]
    sh0 = mag[0:1] * gm0 / (norm[0:1] * norm[0:1])
    sh1 = mag[1:2] * gm1 / (norm[1:2] * norm[1:2])
    rows = iota((16, 128), 0)
    extra = jnp.where(
        rows == 0, gm0, jnp.where(rows == 1, gm1, jnp.where(rows == 2, sh0, jnp.where(rows == 3, sh1, 0.0)))
    )
    ag[z, 0:96, :] = (silu * up_val).astype(BF16)
    ag[z, 96:192, :] = (gate_grad * ratio[0:1]).astype(BF16)
    ag[z, 192:288, :] = (up_grad * ratio[1:2]).astype(BF16)
    ag[z, 288:304, :] = total[288:304].astype(BF16)
    ag[z, 304:336, :] = esum[0:32, :].astype(BF16)
    ag[z, 336:352, :] = extra.astype(BF16)

    def ag_copy(t, sub, rightward):
        r0, n = AG_SUBS[sub]
        ssem, rsem, to = (ars, arr, right) if rightward else (als, alr, left)
        chunk = lax.rem(z + NZ - t, NZ) if rightward else lax.rem(z + t, NZ)
        ref = ag.at[chunk, pl.ds(r0, n), :]
        return hop(ref, ref, ssem.at[t * NSUB + sub], rsem.at[t * NSUB + sub], to)

    def ag_arrived(t, sub, rightward):
        r0, n = AG_SUBS[sub]
        ssem, rsem, to = (ars, arr, right) if rightward else (als, alr, left)
        chunk = lax.rem(z + NZ - 1 - t, NZ) if rightward else lax.rem(z + 1 + t, NZ)
        ref = ag.at[chunk, pl.ds(r0, n), :]
        hop(ref, ref, ssem.at[t * NSUB + sub], rsem.at[t * NSUB + sub], to).wait_recv()

    for sub in range(NSUB):
        for rightward in (True, False):
            ag_copy(0, sub, rightward).start()

    @pl.loop(1, 7)
    def _(t):
        for sub in range(NSUB):
            for rightward in (True, False):
                ag_arrived(t - 1, sub, rightward)
                ag_copy(t, sub, rightward).start()

    for sub in range(NSUB):
        ag_arrived(6, sub, True)
        ag_copy(7, sub, True).start()
    for sub in range(NSUB):
        ag_arrived(6, sub, False)
    for sub in range(NSUB):
        ag_arrived(7, sub, True)

    for q in range(8):
        f0 = q * 128
        for h in range(2):
            p = 2 * q + h
            hid[h * 96 : (h + 1) * 96, f0 : f0 + 128] = ag[p, 0:96, :]
            sgu[0, h * 96 : (h + 1) * 96, f0 : f0 + 128] = ag[p, 96:192, :]
            sgu[1, h * 96 : (h + 1) * 96, f0 : f0 + 128] = ag[p, 192:288, :]

    yback[...] = jnp.zeros((2, 512, 256), BF16)
    out = nn(hid[...], dbase[...]).astype(BF16)
    back = (nt(sgu[0], hi[0]) + nt(sgu[1], hi[1])).astype(BF16)
    for h in range(2):
        r = slice(h * 96, (h + 1) * 96)
        yback[h, 0:96, :] = out[r, 0:256]
        yback[h, 128:224, :] = out[r, 256:512]
        yback[h, 256:352, :] = back[r, 0:256]
        yback[h, 384:480, :] = back[r, 256:512]
        send2[h * 32 : (h + 1) * 32] = nn(perm[1], yback[h]).astype(BF16).reshape(32, 16, 256)

    wait2, drain2 = exchange(send2, recv2, s2s, s2r)

    for q in range(8):
        f0 = q * 128
        both = ag[2 * q, 336:352, :].astype(F32) + ag[2 * q + 1, 336:352, :].astype(F32)
        gmag_ref[:, f0 : f0 + 128] = both[0:2]
        rank[64:72, f0 : f0 + 128] = both[0:8]
        rank[0:32, f0 : f0 + 128] = ag[2 * q, 304:336, :].astype(F32)
        rank[32:64, f0 : f0 + 128] = ag[2 * q + 1, 304:336, :].astype(F32)
    for p in range(8):
        lowt[(p // 2) * 16 : (p // 2) * 16 + 16, (p % 2) * 128 : (p % 2) * 128 + 128] = ag[p, 288:304, :]
    for i in range(2):
        shrink = rank[66 + i : 67 + i, :]
        back_t = nt(up_ref[i], sgu[i]).astype(BF16)
        down_t = nn(back_t[:, 0:96], xs[0, 0:96, :]) + nn(back_t[:, 96:192], xs[1, 0:96, :])
        uh, ul = split(up_ref[i].astype(F32) * shrink)
        down_t = down_t - (nt(uh, hi[i]) + nt(uh, lo[i]) + nt(ul, hi[i]))
        gdown_ref[i] = down_t[:, 0:448]
        rows_i = slice(i * 32, (i + 1) * 32)
        grow = nn(lowt[rows_i, 0:96], sgu[i, 0:96, :]) + nn(lowt[rows_i, 128:224], sgu[i, 96:192, :])
        gup_ref[i] = grow - rank[rows_i, :] * shrink

    wait2()
    got = recv2[...].astype(F32)
    g0 = nn(gt_ref[...], got[:, 0:8, :].reshape(512, 256).astype(BF16))
    g1 = nn(gt_ref[...], got[:, 8:16, :].reshape(512, 256).astype(BF16))
    layer_ref[:, 0:256] = g0[0:64].astype(BF16)
    layer_ref[:, 256:448] = g1[0:64, 0:192].astype(BF16)
    igrad_ref[:, 0:256] = g0[64:128].astype(BF16)
    igrad_ref[:, 256:448] = g1[64:128, 0:192].astype(BF16)

    drain1()
    drain2()

    @pl.loop(1, NZ)
    def _(k):
        early(k, z, lax.rem(z + k, NZ)).wait_send()

    @pl.loop(0, 7)
    def _(t):
        for sub in range(NSUB):
            rs_copy(t, sub, True, True)[1].wait_send()
            rs_copy(t, sub, False, True)[1].wait_send()
            ag_copy(t, sub, True).wait_send()
            ag_copy(t, sub, False).wait_send()

    for sub in range(NSUB):
        rs_copy(7, sub, False, True)[1].wait_send()
        ag_copy(7, sub, True).wait_send()


def body(tokens, route_ids, route_weight, out_cot, base_codes, base_scales, adapter_down, adapter_up, magnitude, down_codes, down_scales):
    vmem = pl.BlockSpec(memory_space=pltpu.VMEM)
    hbm = pl.BlockSpec(memory_space=pl.ANY)
    dma = pltpu.SemaphoreType.DMA
    outs = pl.pallas_call(
        kernel,
        out_shape=(
            jax.ShapeDtypeStruct((64, 448), BF16),
            jax.ShapeDtypeStruct((64, 448), BF16),
            jax.ShapeDtypeStruct((2, 32, 448), F32),
            jax.ShapeDtypeStruct((2, 32, 1024), F32),
            jax.ShapeDtypeStruct((2, 1024), F32),
        ),
        in_specs=[vmem, vmem, vmem, vmem, hbm, vmem, vmem, vmem, vmem, hbm, vmem],
        out_specs=(vmem,) * 5,
        scratch_shapes=[
            pltpu.VMEM((2, 448, 1024), BF16),
            pltpu.VMEM((1024, 448), BF16),
            pltpu.VMEM((2, 512, 1024), BF16),
            pltpu.VMEM((2, 512, 1024), BF16),
            pltpu.VMEM((1024, 512), BF16),
            pltpu.VMEM((128, 512), BF16),
            pltpu.VMEM((128, 512), F32),
            pltpu.VMEM((2, 128, 1024), BF16),
            pltpu.VMEM((2, 512, 512), BF16),
            pltpu.VMEM((128, 512), BF16),
            pltpu.VMEM((16, 1024), F32),
            pltpu.VMEM((64, 512), BF16),
            pltpu.VMEM((NE, 16, 256), BF16),
            pltpu.VMEM((NE, 16, 256), BF16),
            pltpu.VMEM((NE, 16, 256), BF16),
            pltpu.VMEM((NE, 16, 256), BF16),
            pltpu.VMEM((2, 128, 512), BF16),
            pltpu.VMEM((2, 128, 512), BF16),
            pltpu.VMEM((2, 512, 256), BF16),
            pltpu.VMEM((NZ, 48, 128), BF16),
            pltpu.VMEM((NZ, 48, 128), BF16),
            pltpu.VMEM((NZ, RS_ROWS, 128), BF16),
            pltpu.VMEM((7, RS_ROWS, 128), BF16),
            pltpu.VMEM((8, RS_ROWS, 128), BF16),
            pltpu.VMEM((NZ, AG_ROWS, 128), BF16),
            pltpu.VMEM((192, 1024), BF16),
            pltpu.VMEM((2, 192, 1024), BF16),
            pltpu.VMEM((64, 256), BF16),
            pltpu.VMEM((72, 1024), F32),
            dma((2,)),
            dma((NE,)),
            dma((NE,)),
            dma((NE,)),
            dma((NE,)),
            dma((NZ,)),
            dma((NZ,)),
            dma((7 * NSUB,)),
            dma((7 * NSUB,)),
            dma((8 * NSUB,)),
            dma((8 * NSUB,)),
            dma((8 * NSUB,)),
            dma((8 * NSUB,)),
            dma((7 * NSUB,)),
            dma((7 * NSUB,)),
        ],
        compiler_params=pltpu.CompilerParams(
            collective_id=0, has_side_effects=True, vmem_limit_bytes=56 * 1024 * 1024
        ),
    )(
        tokens,
        route_ids,
        route_weight,
        out_cot,
        base_codes[0],
        base_scales.reshape(16, 448),
        adapter_down.reshape(64, 448),
        adapter_up[0],
        magnitude[0],
        down_codes[0],
        down_scales[0],
    )
    layer_out, input_grad, grad_down, grad_up, grad_mag = outs
    return (layer_out, input_grad, grad_down[None], grad_up[None], grad_mag[None])


def solution(mesh):
    in_specs = (
        P("expert", "dp"),
        P("expert", None),
        P("expert", None),
        P("expert", "dp"),
        P("expert", None, "dp", None),
        P("expert", None, None, "dp"),
        P("expert", None, None, "dp"),
        P("expert", None, None, None),
        P("expert", None, None),
        P("expert", None, "dp"),
        P("expert", None, "dp"),
    )
    out_specs = (
        P("expert", "dp"),
        P("expert", "dp"),
        P("expert", None, None, "dp"),
        P("expert", None, None, None),
        P("expert", None, None),
    )
    return jax.shard_map(body, mesh=mesh, in_specs=in_specs, out_specs=out_specs, check_vma=False)
```

time: 368 us -> 129 us (0.35)
  blocking collectives: 148 us -> 0 us
  Pallas kernels: 0 us -> 115 us
  starting transfers between devices: 92 us -> 0 us
  waiting for transfers between devices: 60.9 us -> 0 us
  matrix products: 25.7 us -> 0 us
  between operations: 15.8 us -> 0.64 us
  local copies, waits for them, and re-layouts: 19.3 us -> 12.5 us
  other arithmetic: 5.97 us -> 0 us
    pallas_call x0 -> x1, Pallas kernels: none -> 115 us  [body(): pl.pallas_call(kernel, out_shape=(jax.ShapeDtypeStruct((64, 448), BF16),...]
    all_to_all x4 -> x0, starting transfers between devices: 79 us -> none  [the longest x1 33.5 us: body(): lax.all_to_all(slot_grad.reshape(experts, CAP, local_width), 'expert', sp...]
    psum x2 -> x0, blocking collectives: 65.2 us -> none  [the longest x1 42.9 us: body(): lax.psum(col_part.astype(jnp.bfloat16), 'dp').astype(jnp.float32)]
    all_gather x2 -> x0, blocking collectives: 48.8 us -> none  [the longest x1 24.5 us: body(): lax.all_gather((pre_grad * mag_ratio[None]).astype(jnp.bfloat16), 'dp', a...]
    unnamed x6 -> x0, waiting for transfers between devices: 43.5 us -> none
    unnamed x1 -> x0, blocking collectives: 33.6 us -> none
    dot_general x14 -> x0, matrix products: 25.7 us -> none  [the longest x1 5.26 us: body(): jnp.einsum('irf,idf->ird', adapter_up[0].astype(jnp.float32) * shrink[:,...]
    all_to_all x4 -> x0, waiting for transfers between devices: 17.4 us -> none  [the longest x1 10.1 us: body(): lax.all_to_all(expert_out.reshape(experts, CAP, local_width), 'expert', s...]
  transfers between devices with their start and end apart: 9 -> 0, of which waited for: 3 -> 0; matrix products, arithmetic and copies ran while one was open for 20% -> 0% of each run, Pallas kernels for 0% -> 0%
where the time goes in v1:
time: 129 us; the launch traced here: 128 us
  Pallas kernels  115 us (89%)
  local copies, waits for them, and re-layouts  12.5 us (10%)
    pallas_call x1, Pallas kernels, body(): pl.pallas_call(kernel, out_shape=(jax.ShapeDtypeStruct((64, 448), BF16),...  115 us
    unnamed x8, local copies, waits for them, and re-layouts  12.5 us

profile of v1, /device:TPU:1, one launch (start us, length us, event | category | flops | bytes accessed | tf_op | source)
XLA Modules:
  0.0 128.1 jit_solution(15846847590718633611)
XLA Ops:
  0.6 1.4 %copy.18.w_ref = bf16[64,8]{1,0:T(8,128)(2,1)} copy(bf16[64,8]{0,1:T(8,128)(2,1)} %param.13) | data formatting | bytes 2048 | tf_op args[2]
  2.0 1.4 %copy.17.ids_ref = s32[64,8]{1,0:T(8,128)} copy(s32[64,8]{0,1:T(8,128)} %param.12) | data formatting | bytes 4096 | tf_op args[1]
  3.4 2.3 %copy.16 = bf16[1,1024,448]{2,1,0:T(8,128)(2,1)} copy(bf16[1,1024,448]{1,2,0:T(8,128)(2,1)} %param.20) | data formatting | bytes 1835008 | tf_op args[9]
  5.6 115.0 %shard_map.146 = (bf16[64,448]{1,0:T(8,128)(2,1)}, bf16[64,448]{1,0:T(8,128)(2,1)}, f32[2,32,448]{2,1,0:T(8,128)}, f32[2,32,1024]{2,1,0:T(8,128)}, f32[2,1024]{1,0:T(2,128)}) custom-call(bf16[64,448]{1,0:T(8,128)(2,1)} %tok_ref.1, s32[64,8]{1,0:T(8,128)} %copy.17.ids_ref, bf16[64,8]{1,0:T(8,128)(2,1)} %copy.18.w_ref, bf16[64,448]{1,0:T(8,128)(2,1)} %cot_ref.1, ...), custom_call_target="tpu_custom_call" | custom-call | tf_op jit(solution)/shard_map/pallas_call | solution.py:493
  120.6 1.5 %copy.24 = bf16[64,448]{1,0:T(8,128)(2,1)} copy(bf16[64,448]{1,0:T(8,128)(2,1)} %get-tuple-element.20) | data formatting | bytes 114688
  122.1 1.5 %copy.25 = bf16[64,448]{1,0:T(8,128)(2,1)} copy(bf16[64,448]{1,0:T(8,128)(2,1)} %get-tuple-element.21) | data formatting | bytes 114688
  123.6 1.6 %copy.26 = f32[1,2,32,448]{3,2,1,0:T(8,128)} copy(f32[1,2,32,448]{3,2,1,0:T(8,128)} %bitcast.14) | data formatting | bytes 229376
  125.1 1.7 %copy.27 = f32[1,2,32,1024]{3,2,1,0:T(8,128)} copy(f32[1,2,32,1024]{3,2,1,0:T(8,128)} %bitcast.12) | data formatting | bytes 524288
  126.8 1.3 %copy.28 = f32[1,2,1024]{2,1,0:T(2,128)} copy(f32[1,2,1024]{2,1,0:T(2,128)} %bitcast.19) | data formatting | bytes 16384

commit v2 on v1

v2 whole, which is shorter than its diff:
```python
import jax
import jax.numpy as jnp
from jax import lax
from jax.experimental import pallas as pl
from jax.experimental.pallas import tpu as pltpu
from jax.sharding import PartitionSpec as P

EPSILON = 1e-06
MESH = pl.DeviceIdType.MESH
F32 = jnp.float32
BF16 = jnp.bfloat16
NZ = 16
NE = 64
A_SUBS = ((0, 48), (48, 48), (96, 48), (144, 64))
B_SUBS = ((0, 48), (48, 48))
H_SUBS = ((0, 48), (48, 48), (96, 48))
S_SUBS = ((0, 48), (48, 48), (96, 48), (144, 64))


def nn(a, b):
    return jnp.dot(a, b, preferred_element_type=F32)


def nt(a, b):
    return lax.dot_general(a, b, (((1,), (1,)), ((), ())), preferred_element_type=F32)


def iota(shape, dim):
    return lax.broadcasted_iota(jnp.int32, shape, dim)


def split(v):
    hi = v.astype(BF16)
    return hi, (v - hi.astype(F32)).astype(BF16)


def kernel(
    tok_ref,
    ids_ref,
    w_ref,
    cot_ref,
    codes_hbm,
    scales_ref,
    down_ref,
    up_ref,
    mag_ref,
    dcodes_hbm,
    dscales_ref,
    layer_ref,
    igrad_ref,
    gdown_ref,
    gup_ref,
    gmag_ref,
    codes,
    dcodes,
    hi,
    lo,
    dbase,
    xin,
    xcot,
    tpose,
    upad,
    perm,
    gtc,
    gtw,
    colsq,
    dpad,
    send_in,
    recv_in,
    send_cot,
    recv_cot,
    send_out,
    recv_out,
    send_grad,
    recv_grad,
    xs,
    cs,
    yout,
    ygrad,
    eown,
    erecv,
    a_own,
    a_right,
    a_left,
    b_own,
    b_right,
    b_left,
    a_sum,
    ag_h,
    ag_s,
    hid,
    sgu,
    lowt,
    rank,
    wsem,
    in_s,
    in_r,
    cot_s,
    cot_r,
    out_s,
    out_r,
    grad_s,
    grad_r,
    es,
    er,
    a_rs,
    a_rr,
    a_ls,
    a_lr,
    b_rs,
    b_rr,
    b_ls,
    b_lr,
    h_rs,
    h_rr,
    h_ls,
    h_lr,
    s_rs,
    s_rr,
    s_ls,
    s_lr,
):
    me = lax.axis_index("expert")
    z = lax.axis_index("dp")
    mx = lax.div(me, 16)
    my = lax.rem(lax.div(me, 2), 8)
    mc = lax.rem(me, 2)
    right = lax.rem(z + 1, NZ)
    left = lax.rem(z + NZ - 1, NZ)
    mate = me + 1 - 2 * mc

    wcopy = pltpu.make_async_copy(codes_hbm, codes, wsem.at[0])
    dcopy = pltpu.make_async_copy(dcodes_hbm, dcodes, wsem.at[1])
    wcopy.start()
    dcopy.start()

    def chip_of(o):
        px = lax.rem(mx + lax.div(o, 8), 4)
        py = lax.rem(my + lax.rem(o, 8), 8)
        return (px * 8 + py) * 2

    def for_peers(fn, lo_chip=0, hi_chip=32):
        if lo_chip == 0:
            fn(1, mate)

        @pl.loop(max(lo_chip, 1), hi_chip)
        def _(o):
            chip = chip_of(o)
            fn(2 * o, chip + mc)
            fn(2 * o + 1, chip + 1 - mc)

    barrier = pltpu.get_barrier_semaphore()
    for_peers(
        lambda k, peer: pl.semaphore_signal(
            barrier, inc=1, device_id={"expert": peer}, device_id_type=MESH
        )
    )

    @pl.loop(1, NZ)
    def _(k):
        pl.semaphore_signal(
            barrier, inc=1, device_id={"dp": lax.rem(z + k, NZ)}, device_id_type=MESH
        )

    dup = jnp.where((iota((64, 128), 1) & 63) == iota((64, 128), 0), 1.0, 0.0).astype(BF16)
    ids2 = nn(ids_ref[...].astype(F32).astype(BF16), dup)
    w2 = nn(w_ref[...], dup)
    shape = (512, 128)
    row = iota(shape, 0)
    col = iota(shape, 1)
    exp_of = lax.shift_right_logical(row, 3).astype(F32)
    present = jnp.zeros(shape, F32)
    wt = jnp.zeros(shape, F32)
    for k in range(8):
        match = ids2[k : k + 1, :] == exp_of
        present = present + jnp.where(match, 1.0, 0.0)
        wt = wt + jnp.where(match, w2[k : k + 1, :], 0.0)
    ti = iota((128, 128), 0)
    tj = iota((128, 128), 1)
    tri = jnp.where((ti < tj) & ((tj >= 64) == (ti >= 64)), 1.0, 0.0).astype(BF16)
    position = nn(present.astype(BF16), tri)
    slot = (row & 3).astype(F32)
    same_half = (lax.shift_right_logical(row, 2) & 1) == lax.shift_right_logical(col, 6)
    choose = jnp.where((present > 0.5) & (position == slot) & same_half, 1.0, 0.0)
    chosen_w = choose * wt

    def stack(dst, src):
        dst[64:128, 128:256] = jnp.zeros((64, 128), BF16)
        dst[0:64, :] = src[:, 0:256]
        dst[64:128, 0:192] = src[:, 256:448]

    stack(xin, tok_ref)
    stack(xcot, cot_ref)
    send_in[...] = nn(choose.astype(BF16), xin[...]).reshape(NE, 8, 256).astype(BF16)
    send_cot[...] = nn(chosen_w.astype(BF16), xcot[...]).reshape(NE, 8, 256).astype(BF16)

    pl.semaphore_wait(barrier, NE - 1 + NZ - 1)

    class Exchange:
        def __init__(self, src, dst, ssem, rsem):
            self.src, self.dst, self.ssem, self.rsem = src, dst, ssem, rsem

        def copy(self, k, slot, peer):
            return pltpu.make_async_remote_copy(
                src_ref=self.src.at[peer],
                dst_ref=self.dst.at[slot],
                send_sem=self.ssem.at[k],
                recv_sem=self.rsem.at[slot],
                device_id={"expert": peer},
                device_id_type=MESH,
            )

        def start(self, lo_chip=0, hi_chip=32):
            for_peers(lambda k, peer: self.copy(k, me, peer).start(), lo_chip, hi_chip)

        def keep(self):
            self.dst[me] = self.src[me]

        def wait(self):
            for_peers(lambda k, peer: self.copy(k, peer, peer).wait_recv())

        def drain(self):
            for_peers(lambda k, peer: self.copy(k, me, peer).wait_send())

    x_in = Exchange(send_in, recv_in, in_s, in_r)
    x_cot = Exchange(send_cot, recv_cot, cot_s, cot_r)
    x_out = Exchange(send_out, recv_out, out_s, out_r)
    x_grad = Exchange(send_grad, recv_grad, grad_s, grad_r)
    x_in.start()
    x_cot.start()
    x_in.keep()
    x_cot.keep()

    tpose[88:128, :] = jnp.zeros((40, 512), F32)
    tpose[0:88, 384:512] = jnp.zeros((88, 128), F32)
    tpose[0:16, 0:448] = scales_ref[...]
    tpose[16:80, 0:448] = down_ref[...].astype(F32)
    tpose[80:88, 0:448] = dscales_ref[...]
    dpad[:, 384:512] = jnp.zeros((64, 128), BF16)
    dpad[:, 0:448] = down_ref[...]
    turned = tpose[...].T
    for i in range(4):
        tpose[:, i * 128 : (i + 1) * 128] = turned[i * 128 : (i + 1) * 128, :]
    upad[...] = jnp.zeros((2, 128, 1024), BF16)
    upad[0, 16:48, :] = up_ref[0]
    upad[1, 48:80, :] = up_ref[1]
    hi[:, 448:512, :] = jnp.zeros((2, 64, 1024), BF16)
    lo[:, 448:512, :] = jnp.zeros((2, 64, 1024), BF16)
    dbase[448:512, :] = jnp.zeros((64, 1024), BF16)
    colsq[...] = jnp.zeros((16, 1024), F32)
    wcopy.wait()

    def turned_rows(blk):
        d0 = blk * 64
        return tpose[d0 % 128 : d0 % 128 + 64, (d0 // 128) * 128 : (d0 // 128) * 128 + 128]

    for blk in range(7):
        d0 = blk * 64
        turn = turned_rows(blk)
        turn_b = turn.astype(BF16)
        for i in range(2):
            for fb in range(8):
                f0 = fb * 128
                scale = turn[:, i * 8 + fb : i * 8 + fb + 1]
                val = codes[i, d0 : d0 + 64, f0 : f0 + 128].astype(F32) * scale
                val = val + nn(turn_b, upad[i, :, f0 : f0 + 128])
                top, bottom = split(val)
                hi[i, d0 : d0 + 64, f0 : f0 + 128] = top
                lo[i, d0 : d0 + 64, f0 : f0 + 128] = bottom
                sq = (val * val).reshape(8, 8, 128).sum(axis=0)
                colsq[i * 8 : i * 8 + 8, f0 : f0 + 128] = colsq[i * 8 : i * 8 + 8, f0 : f0 + 128] + sq

    for q in range(8):
        f0 = q * 128
        c0 = jnp.sum(colsq[0:8, f0 : f0 + 128], axis=0, keepdims=True)
        c1 = jnp.sum(colsq[8:16, f0 : f0 + 128], axis=0, keepdims=True)
        rows = iota((16, 128), 0)
        cblock = jnp.where(rows == 0, c0, jnp.where(rows == 1, c1, 0.0)).astype(BF16)
        for h in range(2):
            dn = dpad[h * 32 : (h + 1) * 32, :]
            proj = nn(dn, hi[h, :, f0 : f0 + 128]) + nn(dn, lo[h, :, f0 : f0 + 128])
            eown[2 * q + h, 0:32, :] = proj.astype(BF16)
            eown[2 * q + h, 32:48, :] = cblock

    def early(k, slot, peer):
        return pltpu.make_async_remote_copy(
            src_ref=eown.at[peer],
            dst_ref=erecv.at[slot],
            send_sem=es.at[k],
            recv_sem=er.at[slot],
            device_id={"dp": peer},
            device_id_type=MESH,
        )

    @pl.loop(1, NZ)
    def _(k):
        early(k, z, lax.rem(z + k, NZ)).start()

    pr = iota((256, 256), 0)
    pc = iota((256, 256), 1)

    def target(v):
        return (
            8 * (v & 31)
            + (lax.shift_right_logical(v, 5) & 3)
            + 4 * lax.shift_right_logical(v, 7)
        )

    perm[0] = jnp.where(pc == target(pr), 1.0, 0.0).astype(BF16)
    perm[1] = jnp.where(pr == target(pc), 1.0, 0.0).astype(BF16)
    for p in range(8, NZ):
        a_own[p, 192:208, :] = jnp.zeros((16, 128), BF16)
    yout[...] = jnp.zeros((2, 256, 256), BF16)
    ygrad[...] = jnp.zeros((2, 256, 256), BF16)

    dcopy.wait()
    for blk in range(7):
        d0 = blk * 64
        turn = turned_rows(blk)
        for fb in range(8):
            f0 = fb * 128
            dbase[d0 : d0 + 64, f0 : f0 + 128] = (
                dcodes[d0 : d0 + 64, f0 : f0 + 128].astype(F32) * turn[:, 80 + fb : 81 + fb]
            ).astype(BF16)
    gtc[...] = choose.T.astype(BF16)
    gtw[...] = chosen_w.T.astype(BF16)

    def arrange(recv, dst):
        for h in range(2):
            block = recv[h * 32 : (h + 1) * 32].astype(F32).reshape(256, 256).astype(BF16)
            got = nn(perm[0], block).astype(BF16)
            dst[h, :, 0:256] = got[0:128]
            dst[h, :, 256:512] = got[128:256]

    def lanes_of(c):
        return pl.ds(pl.multiple_of(lax.div(c, 2) * 128, 128), 128)

    def chunk_a(c):
        h = lax.rem(c, 2)
        rows = xs[h, 0:96, :]
        a_own[c, 0:96, :] = nn(rows, hi[0, :, lanes_of(c)]).astype(BF16)
        a_own[c, 96:192, :] = nn(rows, hi[1, :, lanes_of(c)]).astype(BF16)

    def chunk_b(c):
        h = lax.rem(c, 2)
        b_own[c] = nn(cs[h, 0:96, :], dbase[:, lanes_of(c)]).astype(BF16)

    def hop(src, dst, ssem, rsem, to):
        return pltpu.make_async_remote_copy(
            src_ref=src,
            dst_ref=dst,
            send_sem=ssem,
            recv_sem=rsem,
            device_id={"dp": to},
            device_id_type=MESH,
        )

    class Reduce:
        def __init__(self, own, bufs, sems, subs, make):
            self.own, self.bufs, self.sems, self.subs, self.make = own, bufs, sems, subs, make

        def chunk(self, t, d):
            return lax.rem(z + 7 - t, NZ) if d == 0 else lax.rem(z + 8 + t, NZ)

        def copy(self, t, sub, d, first):
            r0, n = self.subs[sub]
            buf, (ssem, rsem) = self.bufs[d], self.sems[d]
            rows = pl.ds(r0, n)
            src = self.own.at[self.chunk(t, d), rows, :] if first else buf.at[t - 1, rows, :]
            at = t * len(self.subs) + sub
            return hop(src, buf.at[t, rows, :], ssem.at[at], rsem.at[at], (right, left)[d])

        def begin(self):
            for d in (0, 1):
                self.make(self.chunk(0, d))
                for sub in range(len(self.subs)):
                    self.copy(0, sub, d, True).start()

        def step(self, t, dirs=(0, 1)):
            for d in dirs:
                self.make(self.chunk(t, d))
            for sub in range(len(self.subs)):
                r0, n = self.subs[sub]
                rows = pl.ds(r0, n)
                for d in dirs:
                    buf = self.bufs[d]
                    self.copy(t - 1, sub, d, True).wait_recv()
                    buf[t - 1, rows, :] = (
                        buf[t - 1, rows, :].astype(F32)
                        + self.own[self.chunk(t, d), rows, :].astype(F32)
                    ).astype(BF16)
                    self.copy(t, sub, d, False).start()

        def total(self):
            for sub in range(len(self.subs)):
                self.copy(6, sub, 0, True).wait_recv()
                self.copy(7, sub, 1, True).wait_recv()
            return (
                self.own[z].astype(F32) + self.bufs[0][6].astype(F32) + self.bufs[1][7].astype(F32)
            )

        def drain(self):
            @pl.loop(0, 7)
            def _(t):
                for sub in range(len(self.subs)):
                    self.copy(t, sub, 0, True).wait_send()
                    self.copy(t, sub, 1, True).wait_send()

            for sub in range(len(self.subs)):
                self.copy(7, sub, 1, True).wait_send()

    class Gather:
        def __init__(self, buf, sems, subs):
            self.buf, self.sems, self.subs = buf, sems, subs

        def copy(self, t, sub, d, chunk):
            r0, n = self.subs[sub]
            ssem, rsem = self.sems[d]
            ref = self.buf.at[chunk, pl.ds(r0, n), :]
            at = t * len(self.subs) + sub
            return hop(ref, ref, ssem.at[at], rsem.at[at], (right, left)[d])

        def sent(self, t, sub, d):
            return self.copy(t, sub, d, lax.rem(z + NZ - t, NZ) if d == 0 else lax.rem(z + t, NZ))

        def come(self, t, sub, d):
            return self.copy(
                t, sub, d, lax.rem(z + NZ - 1 - t, NZ) if d == 0 else lax.rem(z + 1 + t, NZ)
            )

        def begin(self):
            for sub in range(len(self.subs)):
                for d in (0, 1):
                    self.sent(0, sub, d).start()

        def step(self, t, dirs=(0, 1)):
            for sub in range(len(self.subs)):
                for d in dirs:
                    self.come(t - 1, sub, d).wait_recv()
                    self.sent(t, sub, d).start()

        def finish(self):
            for sub in range(len(self.subs)):
                self.come(6, sub, 1).wait_recv()
            for sub in range(len(self.subs)):
                self.come(7, sub, 0).wait_recv()

        def drain(self):
            @pl.loop(0, 7)
            def _(t):
                for sub in range(len(self.subs)):
                    self.sent(t, sub, 0).wait_send()
                    self.sent(t, sub, 1).wait_send()

            for sub in range(len(self.subs)):
                self.sent(7, sub, 0).wait_send()

    red_a = Reduce(a_own, (a_right, a_left), ((a_rs, a_rr), (a_ls, a_lr)), A_SUBS, chunk_a)
    red_b = Reduce(b_own, (b_right, b_left), ((b_rs, b_rr), (b_ls, b_lr)), B_SUBS, chunk_b)
    gat_h = Gather(ag_h, ((h_rs, h_rr), (h_ls, h_lr)), H_SUBS)
    gat_s = Gather(ag_s, ((s_rs, s_rr), (s_ls, s_lr)), S_SUBS)

    x_in.wait()
    arrange(recv_in, xs)
    low = nt(dpad[...], xs[...].reshape(256, 512)).astype(BF16)
    for p in range(8):
        a_own[p, 192:208, :] = low[
            (p // 2) * 16 : (p // 2) * 16 + 16, (p % 2) * 128 : (p % 2) * 128 + 128
        ]
    red_a.begin()

    @pl.loop(1, 4)
    def _(t):
        red_a.step(t)

    x_cot.wait()
    arrange(recv_cot, cs)
    red_b.begin()

    @pl.loop(4, 7)
    def _(t):
        red_a.step(t)
        red_b.step(t - 3)

    red_a.step(7, (1,))
    chunk_a(z)
    red_b.step(4)
    chunk_b(z)

    @pl.loop(1, NZ)
    def _(k):
        peer = lax.rem(z + k, NZ)
        early(k, peer, peer).wait_recv()

    erecv[z] = eown[z]
    esum = erecv[0].astype(F32)
    for p in range(1, NZ):
        esum = esum + erecv[p].astype(F32)
    mag = mag_ref[:, lanes_of(z)]
    norm = jnp.sqrt(esum[32:34, :] + EPSILON)
    ratio = mag / norm

    total = red_a.total()
    a_sum[...] = total
    gate_val = total[0:96] * ratio[0:1]
    up_val = total[96:192] * ratio[1:2]
    ag_h[z, 0:96, :] = (gate_val * jax.nn.sigmoid(gate_val) * up_val).astype(BF16)
    ag_h[z, 96:112, :] = total[192:208].astype(BF16)
    ag_h[z, 112:144, :] = esum[0:32, :].astype(BF16)
    gat_h.begin()

    @pl.loop(5, 7)
    def _(t):
        red_b.step(t)
        gat_h.step(t - 4)

    red_b.step(7, (1,))
    gat_h.step(3)

    unit = red_b.total()
    gate_pre, up_pre = a_sum[0:96, :], a_sum[96:192, :]
    gate_val = gate_pre * ratio[0:1]
    up_val = up_pre * ratio[1:2]
    sig = jax.nn.sigmoid(gate_val)
    gate_grad = unit * up_val * sig * (1.0 + gate_val * (1.0 - sig))
    up_grad = unit * (gate_val * sig)
    gm0 = jnp.sum(gate_grad * gate_pre, axis=0, keepdims=True) / norm[0:1]
    gm1 = jnp.sum(up_grad * up_pre, axis=0, keepdims=True) / norm[1:2]
    sh0 = mag[0:1] * gm0 / (norm[0:1] * norm[0:1])
    sh1 = mag[1:2] * gm1 / (norm[1:2] * norm[1:2])
    rows = iota((16, 128), 0)
    extra = jnp.where(
        rows == 0, gm0, jnp.where(rows == 1, gm1, jnp.where(rows == 2, sh0, jnp.where(rows == 3, sh1, 0.0)))
    )
    ag_s[z, 0:96, :] = (gate_grad * ratio[0:1]).astype(BF16)
    ag_s[z, 96:192, :] = (up_grad * ratio[1:2]).astype(BF16)
    ag_s[z, 192:208, :] = extra.astype(BF16)
    gat_s.begin()

    @pl.loop(4, 7)
    def _(t):
        gat_h.step(t)
        gat_s.step(t - 3)

    gat_h.step(7, (0,))
    gat_s.step(4)
    gat_h.finish()

    def give_back(value, y, send):
        for h in range(2):
            r = slice(h * 96, (h + 1) * 96)
            y[h, 0:96, :] = value[r, 0:256]
            y[h, 128:224, :] = value[r, 256:512]
            send[h * 32 : (h + 1) * 32] = nn(perm[1], y[h]).reshape(32, 8, 256).astype(BF16)

    for q in range(8):
        f0 = q * 128
        for h in range(2):
            hid[h * 96 : (h + 1) * 96, f0 : f0 + 128] = ag_h[2 * q + h, 0:96, :]
    give_back(nt(hid[...], dbase[...]).astype(BF16), yout, send_out)
    gat_s.step(5)
    x_out.start(0, 16)
    gat_s.step(6)
    x_out.start(16, 32)
    gat_s.step(7, (0,))
    x_out.keep()
    gat_s.finish()

    for q in range(8):
        f0 = q * 128
        for h in range(2):
            sgu[0, h * 96 : (h + 1) * 96, f0 : f0 + 128] = ag_s[2 * q + h, 0:96, :]
            sgu[1, h * 96 : (h + 1) * 96, f0 : f0 + 128] = ag_s[2 * q + h, 96:192, :]
    give_back((nt(sgu[0], hi[0]) + nt(sgu[1], hi[1])).astype(BF16), ygrad, send_grad)
    x_grad.start()
    x_grad.keep()

    for q in range(8):
        f0 = q * 128
        both = ag_s[2 * q, 192:208, :].astype(F32) + ag_s[2 * q + 1, 192:208, :].astype(F32)
        gmag_ref[:, f0 : f0 + 128] = both[0:2]
        rank[64:72, f0 : f0 + 128] = both[0:8]
        rank[0:32, f0 : f0 + 128] = ag_h[2 * q, 112:144, :].astype(F32)
        rank[32:64, f0 : f0 + 128] = ag_h[2 * q + 1, 112:144, :].astype(F32)
    for p in range(8):
        lowt[(p // 2) * 16 : (p // 2) * 16 + 16, (p % 2) * 128 : (p % 2) * 128 + 128] = ag_h[p, 96:112, :]
    for i in range(2):
        shrink = rank[66 + i : 67 + i, :]
        back_t = nt(up_ref[i], sgu[i]).astype(BF16)
        down_t = nn(back_t[:, 0:96], xs[0, 0:96, :]) + nn(back_t[:, 96:192], xs[1, 0:96, :])
        uh, ul = split(up_ref[i].astype(F32) * shrink)
        down_t = down_t - (nt(uh, hi[i]) + nt(uh, lo[i]) + nt(ul, hi[i]))
        gdown_ref[i] = down_t[:, 0:448]
        rows_i = slice(i * 32, (i + 1) * 32)
        grow = nn(lowt[rows_i, 0:96], sgu[i, 0:96, :]) + nn(lowt[rows_i, 128:224], sgu[i, 96:192, :])
        gup_ref[i] = grow - rank[rows_i, :] * shrink

    x_in.drain()
    x_cot.drain()
    red_a.drain()
    red_b.drain()
    gat_h.drain()
    gat_s.drain()

    @pl.loop(1, NZ)
    def _(k):
        early(k, z, lax.rem(z + k, NZ)).wait_send()

    def combine(exchange, mat, recv, out):
        exchange.wait()
        got = nn(mat[...], recv[...].astype(F32).reshape(512, 256).astype(BF16)).astype(BF16)
        out[:, 0:256] = got[0:64]
        out[:, 256:448] = got[64:128, 0:192]

    combine(x_out, gtw, recv_out, layer_ref)
    combine(x_grad, gtc, recv_grad, igrad_ref)
    x_out.drain()
    x_grad.drain()


def emit(*refs):
    for src, dst in zip(refs[:5], refs[5:]):
        dst[...] = src[...]


def body(tokens, route_ids, route_weight, out_cot, base_codes, base_scales, adapter_down, adapter_up, magnitude, down_codes, down_scales):
    vmem = pl.BlockSpec(memory_space=pltpu.VMEM)
    hbm = pl.BlockSpec(memory_space=pl.ANY)
    dma = pltpu.SemaphoreType.DMA
    block = pltpu.VMEM((NE, 8, 256), BF16)
    out_shape = (
        jax.ShapeDtypeStruct((64, 448), BF16),
        jax.ShapeDtypeStruct((64, 448), BF16),
        jax.ShapeDtypeStruct((2, 32, 448), F32),
        jax.ShapeDtypeStruct((2, 32, 1024), F32),
        jax.ShapeDtypeStruct((2, 1024), F32),
    )
    outs = pl.pallas_call(
        kernel,
        out_shape=out_shape,
        in_specs=[vmem, vmem, vmem, vmem, hbm, vmem, vmem, vmem, vmem, hbm, vmem],
        out_specs=(vmem,) * 5,
        scratch_shapes=[
            pltpu.VMEM((2, 448, 1024), BF16),
            pltpu.VMEM((448, 1024), BF16),
            pltpu.VMEM((2, 512, 1024), BF16),
            pltpu.VMEM((2, 512, 1024), BF16),
            pltpu.VMEM((512, 1024), BF16),
            pltpu.VMEM((128, 256), BF16),
            pltpu.VMEM((128, 256), BF16),
            pltpu.VMEM((128, 512), F32),
            pltpu.VMEM((2, 128, 1024), BF16),
            pltpu.VMEM((2, 256, 256), BF16),
            pltpu.VMEM((128, 512), BF16),
            pltpu.VMEM((128, 512), BF16),
            pltpu.VMEM((16, 1024), F32),
            pltpu.VMEM((64, 512), BF16),
            block,
            block,
            block,
            block,
            block,
            block,
            block,
            block,
            pltpu.VMEM((2, 128, 512), BF16),
            pltpu.VMEM((2, 128, 512), BF16),
            pltpu.VMEM((2, 256, 256), BF16),
            pltpu.VMEM((2, 256, 256), BF16),
            pltpu.VMEM((NZ, 48, 128), BF16),
            pltpu.VMEM((NZ, 48, 128), BF16),
            pltpu.VMEM((NZ, 208, 128), BF16),
            pltpu.VMEM((7, 208, 128), BF16),
            pltpu.VMEM((8, 208, 128), BF16),
            pltpu.VMEM((NZ, 96, 128), BF16),
            pltpu.VMEM((7, 96, 128), BF16),
            pltpu.VMEM((8, 96, 128), BF16),
            pltpu.VMEM((208, 128), F32),
            pltpu.VMEM((NZ, 144, 128), BF16),
            pltpu.VMEM((NZ, 208, 128), BF16),
            pltpu.VMEM((192, 1024), BF16),
            pltpu.VMEM((2, 192, 1024), BF16),
            pltpu.VMEM((64, 256), BF16),
            pltpu.VMEM((72, 1024), F32),
            dma((2,)),
            *[dma((NE,)) for _ in range(8)],
            dma((NZ,)),
            dma((NZ,)),
            *[dma((n * len(A_SUBS),)) for n in (7, 7, 8, 8)],
            *[dma((n * len(B_SUBS),)) for n in (7, 7, 8, 8)],
            *[dma((n * len(H_SUBS),)) for n in (8, 8, 7, 7)],
            *[dma((n * len(S_SUBS),)) for n in (8, 8, 7, 7)],
        ],
        compiler_params=pltpu.CompilerParams(
            collective_id=0, has_side_effects=True, vmem_limit_bytes=60 * 1024 * 1024
        ),
    )(
        tokens,
        route_ids.T,
        route_weight.T,
        out_cot,
        base_codes[0],
        base_scales.reshape(16, 448),
        adapter_down.reshape(64, 448),
        adapter_up[0],
        magnitude[0],
        down_codes[0].T,
        down_scales[0],
    )
    layer_out, input_grad, grad_down, grad_up, grad_mag = pl.pallas_call(
        emit,
        out_shape=out_shape,
        in_specs=[vmem] * 5,
        out_specs=(vmem,) * 5,
        compiler_params=pltpu.CompilerParams(vmem_limit_bytes=60 * 1024 * 1024),
    )(*outs)
    return (layer_out, input_grad, grad_down[None], grad_up[None], grad_mag[None])


def solution(mesh):
    in_specs = (
        P("expert", "dp"),
        P("expert", None),
        P("expert", None),
        P("expert", "dp"),
        P("expert", None, "dp", None),
        P("expert", None, None, "dp"),
        P("expert", None, None, "dp"),
        P("expert", None, None, None),
        P("expert", None, None),
        P("expert", None, "dp"),
        P("expert", None, "dp"),
    )
    out_specs = (
        P("expert", "dp"),
        P("expert", "dp"),
        P("expert", None, None, "dp"),
        P("expert", None, None, None),
        P("expert", None, None),
    )
    return jax.shard_map(body, mesh=mesh, in_specs=in_specs, out_specs=out_specs, check_vma=False)
```

time: 129 us -> 122 us (0.946)
  local copies, waits for them, and re-layouts: 12.5 us -> 0 us
  Pallas kernels: 115 us -> 121 us
    unnamed x8 -> x0, local copies, waits for them, and re-layouts: 12.5 us -> none
    pallas_call x1 -> x2, Pallas kernels: 115 us -> 121 us  [the longest x1 119 us: body(): pl.pallas_call(kernel, out_shape=out_shape, in_specs=[vmem, vmem, vmem, v...]
where the time goes in v2:
time: 122 us
  Pallas kernels  121 us (99%)
    pallas_call x1, Pallas kernels, body(): pl.pallas_call(kernel, out_shape=out_shape, in_specs=[vmem, vmem, vmem, v...  119 us

profile of v2, /device:TPU:1, one launch (start us, length us, event | category | flops | bytes accessed | tf_op | source)
XLA Modules:
  0.0 121.6 jit_solution(14044875976296757875)
XLA Ops:
  0.6 119.1 %shard_map.146 = (bf16[64,448]{1,0:T(8,128)(2,1)}, bf16[64,448]{1,0:T(8,128)(2,1)}, f32[2,32,448]{2,1,0:T(8,128)}, f32[2,32,1024]{2,1,0:T(8,128)}, f32[2,1024]{1,0:T(2,128)}) custom-call(bf16[64,448]{1,0:T(8,128)(2,1)} %tok_ref.1, s32[8,64]{1,0:T(8,128)} %bitcast.21, bf16[8,64]{1,0:T(8,128)(2,1)} %bitcast.22, bf16[64,448]{1,0:T(8,128)(2,1)} %cot_ref.1, ...), custom_call_target="tpu_custom_call" | custom-call | tf_op jit(solution)/shard_map/pallas_call | solution.py:638
  119.8 1.9 %shard_map.147 = (bf16[64,448]{1,0:T(8,128)(2,1)}, bf16[64,448]{1,0:T(8,128)(2,1)}, f32[2,32,448]{2,1,0:T(8,128)}, f32[2,32,1024]{2,1,0:T(8,128)}, f32[2,1024]{1,0:T(2,128)}) custom-call(bf16[64,448]{1,0:T(8,128)(2,1)} %get-tuple-element.15.refs_0_, bf16[64,448]{1,0:T(8,128)(2,1)} %get-tuple-element.16.refs_1_, f32[2,32,448]{2,1,0:T(8,128)} %get-tuple-element.17.refs_2_, ...), custom_call_target="tpu_custom_call" | custom-call | tf_op jit(solution)/shard_map/pallas_call | solution.py:710

commit v3 on v2

--- a/solution.py
+++ b/solution.py
@@ -11,10 +11,10 @@
 BF16 = jnp.bfloat16
 NZ = 16
 NE = 64
-A_SUBS = ((0, 48), (48, 48), (96, 48), (144, 64))
-B_SUBS = ((0, 48), (48, 48))
-H_SUBS = ((0, 48), (48, 48), (96, 48))
-S_SUBS = ((0, 48), (48, 48), (96, 48), (144, 64))
+A_SUBS = ((0, 96), (96, 112))
+B_SUBS = ((0, 96),)
+H_SUBS = ((0, 144),)
+S_SUBS = ((0, 96), (96, 112))
 
 
 def nn(a, b):

time: 122 us -> 121 us (level)
  no operation moved by 1% of the time
where the time goes in v3:
time: 121 us
  Pallas kernels  120 us (99%)
    pallas_call x1, Pallas kernels, body(): pl.pallas_call(kernel, out_shape=out_shape, in_specs=[vmem, vmem, vmem, v...  118 us

profile of v3, /device:TPU:1, one launch (start us, length us, event | category | flops | bytes accessed | tf_op | source)
XLA Modules:
  0.0 120.6 jit_solution(3888332681010574463)
XLA Ops:
  0.6 118.1 %shard_map.146 = (bf16[64,448]{1,0:T(8,128)(2,1)}, bf16[64,448]{1,0:T(8,128)(2,1)}, f32[2,32,448]{2,1,0:T(8,128)}, f32[2,32,1024]{2,1,0:T(8,128)}, f32[2,1024]{1,0:T(2,128)}) custom-call(bf16[64,448]{1,0:T(8,128)(2,1)} %tok_ref.1, s32[8,64]{1,0:T(8,128)} %bitcast.21, bf16[8,64]{1,0:T(8,128)(2,1)} %bitcast.22, bf16[64,448]{1,0:T(8,128)(2,1)} %cot_ref.1, ...), custom_call_target="tpu_custom_call" | custom-call | tf_op jit(solution)/shard_map/pallas_call | solution.py:638
  118.8 1.9 %shard_map.147 = (bf16[64,448]{1,0:T(8,128)(2,1)}, bf16[64,448]{1,0:T(8,128)(2,1)}, f32[2,32,448]{2,1,0:T(8,128)}, f32[2,32,1024]{2,1,0:T(8,128)}, f32[2,1024]{1,0:T(2,128)}) custom-call(bf16[64,448]{1,0:T(8,128)(2,1)} %get-tuple-element.15.refs_0_, bf16[64,448]{1,0:T(8,128)(2,1)} %get-tuple-element.16.refs_1_, f32[2,32,448]{2,1,0:T(8,128)} %get-tuple-element.17.refs_2_, ...), custom_call_target="tpu_custom_call" | custom-call | tf_op jit(solution)/shard_map/pallas_call | solution.py:710
